TPU v7x, 32 devices: a whole 2x2x4 slice. The times are simulated.
32 devices in a mesh: cluster: 4 (over y, core), sub: 8 (over z, x).
Axes of the slice: x: 2, y: 2, z: 4, core: 2. Of those that a mesh axis runs over, the one named last changes fastest.
Arguments:
- load: float32 [57344, 256], P(('cluster', 'sub'))
- schur: float32 [57344, 1792], P(('cluster', 'sub')), as said below
- modes: float32 [57344, 128], P(('cluster', 'sub')), may hold values from -0.125 to 0.125
- coarse_inverse: float32 [4096, 1024], P(('cluster', 'sub')), as said below
- interface_rows: int32 [32], P(('cluster', 'sub')), may hold values from 896 to 1792, as said below
- mode_count: int32 [32], P(('cluster', 'sub')), may hold values from 64 to 128, as said below
- left_rows: int32 [32, 384], P(('cluster', 'sub')), may hold values from 0 to 1792, as said below
- right_rows: int32 [32, 384], P(('cluster', 'sub')), may hold values from 0 to 1792, as said below
Outputs:
- solution: float32 [57344, 256], P(('cluster', 'sub'))
- residual: float32 [57344, 256], P(('cluster', 'sub'))
Inputs may be any that keep to these rules, and one draw needn't show every extreme that they name: `interface_rows`: every subdomain has at least half of 1792 live rows, and some subdomain has exactly 1792. `mode_count`: every subdomain has at least half of 128 live modes, and some subdomain has exactly 128. Slot j of right_rows[g] and slot j of left_rows[g + 1] name the same interface unknown; the used slots of a row come first, all other slots hold 1792. Two neighbours share at least half of 384 rows and some pair shares exactly 384. The used entries of left_rows[g] and right_rows[g] are distinct live rows of g. left_rows[0] and right_rows[31] are unused. `right_rows`: see left_rows. `schur`: each block S_g is symmetric positive definite with a positive diagonal. `coarse_inverse`: each cluster's coarse inverse is symmetric positive definite.
All inputs are finite; a program needn't handle non-finite values.
Results may differ from a plain program's by a relative error of at most 0.0001.
Values sent between devices are 32-bit elements; how exact they have to be, the bound alone decides.
No kernel may reach another device: no remote copies, remote signals or barrier semaphores. Data moves between devices by JAX's collectives and lax.ppermute only.
A program may use at most 128 MiB of HBM per device.

v0:
```python
import jax
import jax.numpy as jnp
from jax import lax
from jax.sharding import PartitionSpec as P

ITERS = 3


def passed_along(value, axis, by):
    devices = lax.axis_size(axis)
    pairs = [(i, i + by) for i in range(devices) if 0 <= i + by < devices]
    return lax.ppermute(value, axis, pairs)


def take_rows(field, indices):
    return jnp.take(field, indices, axis=0, mode="fill", fill_value=0.0)


def assemble(field, left_index, right_index):
    to_left = take_rows(field, left_index)
    to_right = take_rows(field, right_index)
    from_left = passed_along(to_right, ("cluster", "sub"), 1)
    from_right = passed_along(to_left, ("cluster", "sub"), -1)
    merged = field.at[left_index].add(from_left, mode="drop")
    return merged.at[right_index].add(from_right, mode="drop")


def local(load, schur, modes, coarse_inverse, interface_rows, mode_count, left_rows, right_rows):
    highest = lax.Precision.HIGHEST
    order = schur.shape[0]
    mode_total = modes.shape[1]
    left_index = left_rows[0]
    right_index = right_rows[0]
    positions = jnp.arange(order, dtype=jnp.int32)
    live = (positions < interface_rows[0]).astype(jnp.float32)
    ones_shared = jnp.ones((left_index.shape[0],), jnp.float32)
    counted = jnp.zeros((order,), jnp.float32).at[left_index].add(ones_shared, mode="drop")
    counted = counted.at[right_index].add(ones_shared, mode="drop")
    share = (live / (1.0 + counted))[:, None]
    live_column = live[:, None]
    mode_live = (jnp.arange(mode_total, dtype=jnp.int32) < mode_count[0]).astype(jnp.float32)[
        :, None
    ]
    schur_diag = jnp.diagonal(schur)[:, None]
    rhs = assemble(live_column * load, left_index, right_index)
    solution = jnp.zeros_like(rhs)
    residual = rhs
    for iteration in range(ITERS):
        modal = jnp.einsum(
            "im,ik->mk",
            modes,
            share * residual,
            precision=highest,
            preferred_element_type=jnp.float32,
        )
        modal = modal * mode_live
        correction = jnp.dot(
            coarse_inverse,
            lax.all_gather(modal, "sub", axis=0, tiled=True),
            precision=highest,
            preferred_element_type=jnp.float32,
        )
        correction = correction * mode_live
        prolonged = jnp.dot(
            modes, correction, precision=highest, preferred_element_type=jnp.float32
        )
        direction = assemble(share * (prolonged + residual / schur_diag), left_index, right_index)
        product = jnp.dot(schur, direction, precision=highest, preferred_element_type=jnp.float32)
        image = assemble(live_column * product, left_index, right_index)
        numerator, denominator = lax.psum(
            (jnp.sum(share * residual * image, axis=0), jnp.sum(share * image * image, axis=0)),
            ("cluster", "sub"),
        )
        alpha = (numerator / (denominator + 1e-06))[None, :]
        solution = solution + alpha * direction
        residual = residual - alpha * image
    return (solution, residual)


def solution(mesh):
    return jax.shard_map(
        local,
        mesh=mesh,
        in_specs=(
            P(("cluster", "sub"), None),
            P(("cluster", "sub"), None),
            P(("cluster", "sub"), None),
            P(("cluster", "sub"), None),
            P(("cluster", "sub")),
            P(("cluster", "sub")),
            P(("cluster", "sub"), None),
            P(("cluster", "sub"), None),
        ),
        out_specs=(P(("cluster", "sub"), None), P(("cluster", "sub"), None)),
        check_vma=False,
    )
```

profile of v0, /device:TPU:10, one launch (start us, length us, event | category | flops | bytes accessed | tf_op | source)
XLA Modules:
  0.0 679.0 jit_solution(7623673633662888873)
XLA Ops:
  13.1 3.4 collective-permute-start
  22.2 3.5 scatter_custom_fusion
  26.4 3.6 scatter_fusion
  30.6 3.9 collective-permute-done
  34.5 5.1 scatter_fusion.1
  39.6 5.1 scatter_fusion.2
  49.5 28.0 %gather_fusion = f32[1792]{0:T(1024)S(1)} fusion(f32[1792,1792]{1,0:T(8,128)} %param.11, s32[1792]{0:T(1024)S(1)} %or_reduce_fusion), kind=kCustom, calls=%fused_computation.14 | custom fusion | bytes 28672 | tf_op jit(solution)/shard_map/jit(diagonal)/cond/branch_0_fun/gather | solution.py:44
  77.4 11.9 %all-gather.4.cloned.1.call-done = f32[1024,256]{0,1:T(8,128)} async-done(((f32[128,256]{0,1:T(8,128)}), f32[1024,256]{0,1:T(8,128)}) %all-gather.4.cloned.1.call-update) | async-done | bytes 1048592 | tf_op jit(solution)/shard_map/all_gather | solution.py:59
  91.5 4.4 add_multiply_fusion.2
  107.6 3.5 collective-permute-start.3
  111.1 11.5 %collective-permute-done.2 = f32[384,256]{1,0:T(8,128)} collective-permute-done((f32[384,256]{1,0:T(8,128)S(1)}, f32[384,256]{1,0:T(8,128)}, u32[]{:S(2)}, u32[]{:S(2)}) %collective-permute-start.2) | collective-permute-done | bytes 393248 | tf_op jit(solution)/shard_map/ppermute | solution.py:12
  122.6 3.8 scatter_fusion.3
  126.4 3.9 scatter_fusion.4
  130.3 27.1 %fusion = f32[1792,256]{0,1:T(8,128)} fusion(f32[1792,256]{1,0:T(8,128)S(1)} %scatter_fusion.4, f32[1792,1792]{1,0:T(8,128)} %param.11, f32[1792]{0:T(1024)S(1)} %fusion.33), kind=kOutput, calls=%fused_computation.40 | convolution fusion | flops 9865461760 | bytes 16522240 | tf_op jit(solution)/shard_map/dot_general | solution.py:68
  160.1 4.1 gather_fusion.6
  164.2 3.7 gather_fusion.5
  172.8 3.9 collective-permute-start.5
  176.7 10.5 %collective-permute-done.4 = f32[384,256]{1,0:T(8,128)} collective-permute-done((f32[384,256]{1,0:T(8,128)S(1)}, f32[384,256]{1,0:T(8,128)}, u32[]{:S(2)}, u32[]{:S(2)}) %collective-permute-start.4) | collective-permute-done | bytes 393248 | tf_op jit(solution)/shard_map/ppermute | solution.py:12
  187.2 5.6 scatter_fusion.5
  192.8 5.6 scatter_fusion.6
  203.6 43.9 %all-reduce.2 = (f32[256]{0:T(256)S(1)}, f32[256]{0:T(256)S(1)}) all-reduce(f32[256]{0:T(256)S(1)} %get-tuple-element.12, f32[256]{0:T(256)S(1)} %get-tuple-element.11), channel_id=1, replica_groups=mesh['cluster'=4,'sub'=8] {'cluster','sub'}, use_global_device_ids=true, to_apply=%region_9.11 | all-reduce | flops 512 | bytes 4096 | tf_op jit(solution)/shard_map/psum | solution.py:70
  253.4 37.5 %all-gather.6.cloned.1.call-done = f32[1024,256]{0,1:T(8,128)} async-done(((f32[128,256]{0,1:T(8,128)}), f32[1024,256]{0,1:T(8,128)}) %all-gather.6.cloned.1.call-update) | async-done | bytes 1048592 | tf_op jit(solution)/shard_map/all_gather | solution.py:59
  293.1 4.4 add_multiply_fusion.1
  300.2 3.7 gather_fusion.8
  303.9 3.7 gather_fusion.7
  316.4 11.7 %collective-permute-done.6 = f32[384,256]{1,0:T(8,128)} collective-permute-done((f32[384,256]{1,0:T(8,128)S(1)}, f32[384,256]{1,0:T(8,128)}, u32[]{:S(2)}, u32[]{:S(2)}) %collective-permute-start.6) | collective-permute-done | bytes 393248 | tf_op jit(solution)/shard_map/ppermute | solution.py:12
  328.0 5.6 scatter_fusion.7
  333.6 5.6 scatter_fusion.8
  339.3 27.7 %fusion.1 = f32[1792,256]{0,1:T(8,128)} fusion(f32[1792,256]{1,0:T(8,128)} %scatter_fusion.8, f32[1792,1792]{1,0:T(8,128)} %param.11, f32[1792]{0:T(1024)S(1)} %fusion.33), kind=kOutput, calls=%fused_computation.41 | convolution fusion | flops 9865461760 | bytes 16522240 | tf_op jit(solution)/shard_map/dot_general | solution.py:68
  369.7 4.1 gather_fusion.10
  373.8 3.7 gather_fusion.9
  382.4 3.9 collective-permute-start.9
  386.3 10.5 %collective-permute-done.8 = f32[384,256]{1,0:T(8,128)} collective-permute-done((f32[384,256]{1,0:T(8,128)S(1)}, f32[384,256]{1,0:T(8,128)}, u32[]{:S(2)}, u32[]{:S(2)}) %collective-permute-start.8) | collective-permute-done | bytes 393248 | tf_op jit(solution)/shard_map/ppermute | solution.py:12
  396.8 5.6 scatter_fusion.9
  402.4 5.6 scatter_fusion.10
  413.2 43.9 %all-reduce.1 = (f32[256]{0:T(256)S(1)}, f32[256]{0:T(256)S(1)}) all-reduce(f32[256]{0:T(256)S(1)} %get-tuple-element.10, f32[256]{0:T(256)S(1)} %get-tuple-element.9), channel_id=1, replica_groups=mesh['cluster'=4,'sub'=8] {'cluster','sub'}, use_global_device_ids=true, to_apply=%region_17.19 | all-reduce | flops 512 | bytes 4096 | tf_op jit(solution)/shard_map/psum | solution.py:70
  462.9 37.5 %all-gather.8.cloned.1.call-done = f32[1024,256]{0,1:T(8,128)} async-done(((f32[128,256]{0,1:T(8,128)}), f32[1024,256]{0,1:T(8,128)}) %all-gather.8.cloned.1.call-update) | async-done | bytes 1048592 | tf_op jit(solution)/shard_map/all_gather | solution.py:59
  502.7 4.4 add_multiply_fusion
  524.4 11.9 %collective-permute-done.10 = f32[384,256]{1,0:T(8,128)S(1)} collective-permute-done((f32[384,256]{1,0:T(8,128)S(1)}, f32[384,256]{1,0:T(8,128)S(1)}, u32[]{:S(2)}, u32[]{:S(2)}) %collective-permute-start.10) | collective-permute-done | bytes 393248 | tf_op jit(solution)/shard_map/ppermute | solution.py:12
  536.3 5.3 scatter_fusion.11
  541.6 5.3 scatter_fusion.12
  547.0 27.7 %fusion.2 = f32[1792,256]{0,1:T(8,128)} fusion(f32[1792,256]{1,0:T(8,128)} %scatter_fusion.12, f32[1792,1792]{1,0:T(8,128)} %param.11, f32[1792]{0:T(1024)S(1)} %fusion.33), kind=kOutput, calls=%fused_computation.42 | convolution fusion | flops 9865461760 | bytes 16522240 | tf_op jit(solution)/shard_map/dot_general | solution.py:68
  588.3 3.9 collective-permute-start.13
  598.5 4.6 collective-permute-done.12
  603.2 5.1 scatter_fusion.13
  608.3 5.1 scatter_fusion.14
  618.2 43.9 %all-reduce = (f32[256]{0:T(256)S(1)}, f32[256]{0:T(256)S(1)}) all-reduce(f32[256]{0:T(256)S(1)} %get-tuple-element.8, f32[256]{0:T(256)S(1)} %get-tuple-element.7), channel_id=1, replica_groups=mesh['cluster'=4,'sub'=8] {'cluster','sub'}, use_global_device_ids=true, to_apply=%region_25.27 | all-reduce | flops 512 | bytes 4096 | tf_op jit(solution)/shard_map/psum | solution.py:70
  662.1 5.6 multiply_subtract_fusion
  (153 shorter events, 129.9 us)
Async XLA Ops:
  7.2 39.4 %copy-start = (f32[1792,128]{1,0:T(8,128)S(1)}, f32[1792,128]{1,0:T(8,128)}, u32[]{:S(2)}) copy-start(f32[1792,128]{1,0:T(8,128)} %param.12) | copy-start | bytes 2752516
  7.2 82.1 %all-gather.4.cloned.1.call-start = ((), (), s32[]{:S(2)}) async-start(), calls=%async_computation | async-start | bytes 1179648 | tf_op jit(solution)/shard_map/all_gather | solution.py:59
  8.0 4.2 copy-start.21
  8.7 1.8 copy-start.15
  10.5 6.1 copy-start.2
  10.5 6.0 copy-start.31
  13.1 21.4 %collective-permute-start = (f32[384,256]{1,0:T(8,128)}, f32[384,256]{1,0:T(8,128)S(1)}, u32[]{:S(2)}, u32[]{:S(2)}) collective-permute-start(f32[384,256]{1,0:T(8,128)} %broadcast_select_fusion.13), channel_id=1, source_target_pairs={{0,1},{1,2},{2,3},{3,4},{4,5},{5,6},{6,7},{7,8},{8,9},{9,10},{10,1... | collective-permute-start | bytes 1179656 | tf_op jit(solution)/shard_map/ppermute | solution.py:12
  16.6 1.9 copy-start.24
  16.6 1.8 copy-start.18
  18.5 21.1 %collective-permute-start.1 = (f32[384,256]{1,0:T(8,128)S(1)}, f32[384,256]{1,0:T(8,128)S(1)}, u32[]{:S(2)}, u32[]{:S(2)}) collective-permute-start(f32[384,256]{1,0:T(8,128)S(1)} %broadcast_select_fusion.12), channel_id=1, source_target_pairs={{1,0},{2,1},{3,2},{4,3},{5,4},{6,5},{7,6},{8,7},{9,8},{10,9},{11,1... | collective-permute-start | bytes 1179656 | tf_op jit(solution)/shard_map/ppermute | solution.py:12
  21.6 12.9 %copy-start.12 = (s32[384]{0:T(512)}, s32[384]{0:T(512)S(1)}, u32[]{:S(2)}) copy-start(s32[384]{0:T(512)S(1)} %fusion.37) | copy-start | bytes 4612
  26.4 13.2 %copy-start.9 = (s32[384]{0:T(512)}, s32[384]{0:T(512)S(1)}, u32[]{:S(2)}) copy-start(s32[384]{0:T(512)S(1)} %fusion.38) | copy-start | bytes 4612
  44.7 1.8 copy-start.26
  46.5 2.3 copy-start.3
  48.9 242.0 %all-gather.6.cloned.1.call-start = ((), (), s32[]{:S(2)}) async-start(), calls=%async_computation.1 | async-start | bytes 1179648 | tf_op jit(solution)/shard_map/all_gather | solution.py:59
  49.4 39.8 %copy-start.8 = (f32[128,1024]{1,0:T(8,128)S(1)}, f32[128,1024]{1,0:T(8,128)}, u32[]{:S(2)}) copy-start(f32[128,1024]{1,0:T(8,128)} %param.13) | copy-start | bytes 1572868
  95.9 1.8 copy-start.19
  97.7 2.2 copy-start.16
  99.9 2.2 copy-start.22
  99.9 5.8 copy-start.25
  99.9 22.7 %copy-start.13 = (s32[384]{0:T(512)S(1)}, s32[384]{0:T(512)}, u32[]{:S(2)}) copy-start(s32[384]{0:T(512)} %copy-done.12) | copy-start | bytes 4612
  103.2 19.4 %collective-permute-start.2 = (f32[384,256]{1,0:T(8,128)S(1)}, f32[384,256]{1,0:T(8,128)}, u32[]{:S(2)}, u32[]{:S(2)}) collective-permute-start(f32[384,256]{1,0:T(8,128)S(1)} %broadcast_select_fusion.11), channel_id=1, source_target_pairs={{0,1},{1,2},{2,3},{3,4},{4,5},{5,6},{6,7},{7,8},{8,9},{9,10},{10,1... | collective-permute-start | bytes 1179656 | tf_op jit(solution)/shard_map/ppermute | solution.py:12
  107.6 18.8 %copy-start.10 = (s32[384]{0:T(512)S(1)}, s32[384]{0:T(512)}, u32[]{:S(2)}) copy-start(s32[384]{0:T(512)} %copy-done.9) | copy-start | bytes 4612
  107.6 18.7 %collective-permute-start.3 = (f32[384,256]{1,0:T(8,128)}, f32[384,256]{1,0:T(8,128)}, u32[]{:S(2)}, u32[]{:S(2)}) collective-permute-start(f32[384,256]{1,0:T(8,128)} %broadcast_select_fusion.10), channel_id=1, source_target_pairs={{1,0},{2,1},{3,2},{4,3},{5,4},{6,5},{7,6},{8,7},{9,8},{10,9},{11,1... | collective-permute-start | bytes 1179656 | tf_op jit(solution)/shard_map/ppermute | solution.py:12
  169.0 18.2 %collective-permute-start.4 = (f32[384,256]{1,0:T(8,128)S(1)}, f32[384,256]{1,0:T(8,128)}, u32[]{:S(2)}, u32[]{:S(2)}) collective-permute-start(f32[384,256]{1,0:T(8,128)S(1)} %broadcast_select_fusion.9), channel_id=1, source_target_pairs={{0,1},{1,2},{2,3},{3,4},{4,5},{5,6},{6,7},{7,8},{8,9},{9,10},{10,1... | collective-permute-start | bytes 1179656 | tf_op jit(solution)/shard_map/ppermute | solution.py:12
  172.8 20.0 %collective-permute-start.5 = (f32[384,256]{1,0:T(8,128)}, f32[384,256]{1,0:T(8,128)}, u32[]{:S(2)}, u32[]{:S(2)}) collective-permute-start(f32[384,256]{1,0:T(8,128)} %broadcast_select_fusion.8), channel_id=1, source_target_pairs={{1,0},{2,1},{3,2},{4,3},{5,4},{6,5},{7,6},{8,7},{9,8},{10,9},{11,1... | collective-permute-start | bytes 1179656 | tf_op jit(solution)/shard_map/ppermute | solution.py:12
  247.5 2.3 copy-start.27
  253.3 247.1 %all-gather.8.cloned.1.call-start = ((), (), s32[]{:S(2)}) async-start(), calls=%async_computation.2 | async-start | bytes 1179648 | tf_op jit(solution)/shard_map/all_gather | solution.py:59
  308.7 19.4 %collective-permute-start.6 = (f32[384,256]{1,0:T(8,128)S(1)}, f32[384,256]{1,0:T(8,128)}, u32[]{:S(2)}, u32[]{:S(2)}) collective-permute-start(f32[384,256]{1,0:T(8,128)S(1)} %broadcast_select_fusion.7), channel_id=1, source_target_pairs={{0,1},{1,2},{2,3},{3,4},{4,5},{5,6},{6,7},{7,8},{8,9},{9,10},{10,1... | collective-permute-start | bytes 1179656 | tf_op jit(solution)/shard_map/ppermute | solution.py:12
  313.0 20.6 %collective-permute-start.7 = (f32[384,256]{1,0:T(8,128)}, f32[384,256]{1,0:T(8,128)}, u32[]{:S(2)}, u32[]{:S(2)}) collective-permute-start(f32[384,256]{1,0:T(8,128)} %broadcast_select_fusion.6), channel_id=1, source_target_pairs={{1,0},{2,1},{3,2},{4,3},{5,4},{6,5},{7,6},{8,7},{9,8},{10,9},{11,1... | collective-permute-start | bytes 1179656 | tf_op jit(solution)/shard_map/ppermute | solution.py:12
  378.6 18.2 %collective-permute-start.8 = (f32[384,256]{1,0:T(8,128)S(1)}, f32[384,256]{1,0:T(8,128)}, u32[]{:S(2)}, u32[]{:S(2)}) collective-permute-start(f32[384,256]{1,0:T(8,128)S(1)} %broadcast_select_fusion.5), channel_id=1, source_target_pairs={{0,1},{1,2},{2,3},{3,4},{4,5},{5,6},{6,7},{7,8},{8,9},{9,10},{10,1... | collective-permute-start | bytes 1179656 | tf_op jit(solution)/shard_map/ppermute | solution.py:12
  382.4 20.0 %collective-permute-start.9 = (f32[384,256]{1,0:T(8,128)}, f32[384,256]{1,0:T(8,128)}, u32[]{:S(2)}, u32[]{:S(2)}) collective-permute-start(f32[384,256]{1,0:T(8,128)} %broadcast_select_fusion.4), channel_id=1, source_target_pairs={{1,0},{2,1},{3,2},{4,3},{5,4},{6,5},{7,6},{8,7},{9,8},{10,9},{11,1... | collective-permute-start | bytes 1179656 | tf_op jit(solution)/shard_map/ppermute | solution.py:12
  457.1 2.3 copy-start.29
  459.4 1.2 copy-start.5
  517.0 19.3 %collective-permute-start.10 = (f32[384,256]{1,0:T(8,128)S(1)}, f32[384,256]{1,0:T(8,128)S(1)}, u32[]{:S(2)}, u32[]{:S(2)}) collective-permute-start(f32[384,256]{1,0:T(8,128)S(1)} %broadcast_select_fusion.3), channel_id=1, source_target_pairs={{0,1},{1,2},{2,3},{3,4},{4,5},{5,6},{6,7},{7,8},{8,9},{9,10},{10,1... | collective-permute-start | bytes 1179656 | tf_op jit(solution)/shard_map/ppermute | solution.py:12
  521.0 20.6 %collective-permute-start.11 = (f32[384,256]{1,0:T(8,128)}, f32[384,256]{1,0:T(8,128)S(1)}, u32[]{:S(2)}, u32[]{:S(2)}) collective-permute-start(f32[384,256]{1,0:T(8,128)} %broadcast_select_fusion.2), channel_id=1, source_target_pairs={{1,0},{2,1},{3,2},{4,3},{5,4},{6,5},{7,6},{8,7},{9,8},{10,9},{11,1... | collective-permute-start | bytes 1179656 | tf_op jit(solution)/shard_map/ppermute | solution.py:12
  574.7 2.7 copy-start.20
  577.4 3.4 copy-start.17
  580.8 3.2 copy-start.23
  584.9 18.3 %collective-permute-start.12 = (f32[384,256]{1,0:T(8,128)}, f32[384,256]{1,0:T(8,128)S(1)}, u32[]{:S(2)}, u32[]{:S(2)}) collective-permute-start(f32[384,256]{1,0:T(8,128)} %broadcast_select_fusion.1), channel_id=1, source_target_pairs={{0,1},{1,2},{2,3},{3,4},{4,5},{5,6},{6,7},{7,8},{8,9},{9,10},{10,1... | collective-permute-start | bytes 1179656 | tf_op jit(solution)/shard_map/ppermute | solution.py:12
  588.3 20.0 %collective-permute-start.13 = (f32[384,256]{1,0:T(8,128)}, f32[384,256]{1,0:T(8,128)S(1)}, u32[]{:S(2)}, u32[]{:S(2)}) collective-permute-start(f32[384,256]{1,0:T(8,128)} %broadcast_select_fusion), channel_id=1, source_target_pairs={{1,0},{2,1},{3,2},{4,3},{5,4},{6,5},{7,6},{8,7},{9,8},{10,9},{11,1... | collective-permute-start | bytes 1179656 | tf_op jit(solution)/shard_map/ppermute | solution.py:12
  593.9 2.9 copy-start.1
  596.8 6.4 copy-start.14
  598.5 9.8 %copy-start.11 = (s32[384]{0:T(512)S(1)}, s32[384]{0:T(512)}, u32[]{:S(2)}) copy-start(s32[384]{0:T(512)} %copy-done.9) | copy-start | bytes 4612
  613.4 2.9 copy-start.6
  616.3 45.8 %copy-start.28 = (f32[256]{0:T(256)S(1)}, f32[256]{0:T(256)}, u32[]{:S(2)}) copy-start(f32[256]{0:T(256)} %copy-done.27) | copy-start | bytes 3076
  616.3 45.8 %copy-start.30 = (f32[256]{0:T(256)S(1)}, f32[256]{0:T(256)}, u32[]{:S(2)}) copy-start(f32[256]{0:T(256)} %copy-done.29) | copy-start | bytes 3076
  667.7 2.9 copy-start.7
  (1 other events, 1.2 us)
Sparse Core Ops, SparseCore 0:
  49.0 40.2 all-gather.3
  253.4 37.3 all-gather.5
  463.0 37.3 all-gather.7
where the time goes:
time: 690 us; the launch traced here: 679 us
  waiting for transfers between devices  152 us (22%)
  blocking collectives  132 us (19%)
  other arithmetic  119 us (17%)
  local copies, waits for them, and re-layouts  111 us (16%)
  matrix products  109 us (16%)
  starting transfers between devices  41.1 us (6%)
  between operations  15.9 us (2%)
    psum x3, blocking collectives, local(): lax.psum((jnp.sum(share * residual * image, axis=0), jnp.sum(share * imag...  132 us
    all_gather x3, waiting for transfers between devices, local(): lax.all_gather(modal, 'sub', axis=0, tiled=True)  86.9 us
    dot_general x3, matrix products, local(): jnp.dot(schur, direction, precision=highest, preferred_element_type=jnp.f...  82.5 us
    ppermute x14, waiting for transfers between devices, passed_along(): return lax.ppermute(value, axis, pairs)  64.6 us
    gather x14, local copies, waits for them, and re-layouts, take_rows(): return jnp.take(field, indices, axis=0, mode='fill', fill_value=0.0)  43.5 us
    ppermute x14, starting transfers between devices, passed_along(): return lax.ppermute(value, axis, pairs)  40.9 us
    scatter-add x7, other arithmetic, assemble(): return merged.at[right_index].add(from_right, mode='drop')  36.3 us
    scatter-add x7, other arithmetic, assemble(): merged = field.at[left_index].add(from_left, mode='drop')  36.1 us
  transfers between devices with their start and end apart: 17, of which 10 were waited for; matrix products, arithmetic and copies ran while one was open for 14% of the time, Pallas kernels for 0%

commit v1 on v0

--- a/solution.py
+++ b/solution.py
@@ -2,6 +2,7 @@
 import jax.numpy as jnp
 from jax import lax
 from jax.sharding import PartitionSpec as P
+from jax.lax import all_to_all, axis_size
 
 ITERS = 3
 
@@ -56,7 +57,15 @@
         modal = modal * mode_live
         correction = jnp.dot(
             coarse_inverse,
-            lax.all_gather(modal, "sub", axis=0, tiled=True),
+            jnp.concatenate(
+                all_to_all(
+                    jnp.stack([modal for _ in range(axis_size("sub"))], axis=0),
+                    "sub",
+                    split_axis=0,
+                    concat_axis=0,
+                ),
+                axis=0,
+            ),
             precision=highest,
             preferred_element_type=jnp.float32,
         )

time: 690 us -> 641 us (0.929)
  waiting for transfers between devices: 152 us -> 65.5 us
  blocking collectives: 132 us -> 181 us
  between operations: 15.9 us -> 3 us
    all_gather x3 -> x0, waiting for transfers between devices: 86.9 us -> none  [local(): lax.all_gather(modal, 'sub', axis=0, tiled=True)]
    all_to_all x0 -> x2, blocking collectives: none -> 54.7 us  [local(): all_to_all(jnp.stack([modal for _ in range(axis_size('sub'))], axis=0), '...]
  transfers between devices with their start and end apart: 17 -> 15, of which waited for: 10 -> 7; matrix products, arithmetic and copies ran while one was open for 14% -> 15% of each run, Pallas kernels for 0% -> 0%
where the time goes in v1:
time: 641 us; the launch traced here: 630 us
  blocking collectives  181 us (28%)
  other arithmetic  119 us (19%)
  local copies, waits for them, and re-layouts  112 us (17%)
  matrix products  103 us (16%)
  waiting for transfers between devices  65.5 us (10%)
  starting transfers between devices  46.3 us (7%)
    psum x3, blocking collectives, local(): lax.psum((jnp.sum(share * residual * image, axis=0), jnp.sum(share * imag...  127 us
    dot_general x3, matrix products, local(): jnp.dot(schur, direction, precision=highest, preferred_element_type=jnp.f...  82.5 us
    ppermute x14, waiting for transfers between devices, passed_along(): return lax.ppermute(value, axis, pairs)  65.5 us
    all_to_all x2, blocking collectives, local(): all_to_all(jnp.stack([modal for _ in range(axis_size('sub'))], axis=0), '...  54.7 us
    gather x14, local copies, waits for them, and re-layouts, take_rows(): return jnp.take(field, indices, axis=0, mode='fill', fill_value=0.0)  43.2 us
    ppermute x14, starting transfers between devices, passed_along(): return lax.ppermute(value, axis, pairs)  41.1 us
    scatter-add x7, other arithmetic, assemble(): return merged.at[right_index].add(from_right, mode='drop')  36.3 us
    scatter-add x7, other arithmetic, assemble(): merged = field.at[left_index].add(from_left, mode='drop')  36.1 us
  transfers between devices with their start and end apart: 15, of which 7 were waited for; matrix products, arithmetic and copies ran while one was open for 15% of the time, Pallas kernels for 0%

profile of v1, /device:TPU:10, one launch (start us, length us, event | category | flops | bytes accessed | tf_op | source)
XLA Modules:
  0.0 630.0 jit_solution(9794008122226122836)
XLA Ops:
  6.5 3.4 collective-permute-start
  15.7 3.5 scatter_custom_fusion
  19.9 3.6 scatter_fusion
  24.0 3.9 collective-permute-done
  27.9 5.1 scatter_fusion.1
  33.0 5.1 scatter_fusion.2
  42.8 5.2 all-to-all-start
  48.5 28.0 %gather_fusion = f32[1792]{0:T(1024)S(1)} fusion(f32[1792,1792]{1,0:T(8,128)} %param.11, s32[1792]{0:T(1024)S(1)} %or_reduce_fusion), kind=kCustom, calls=%fused_computation.14 | custom fusion | bytes 28672 | tf_op jit(solution)/shard_map/jit(diagonal)/cond/branch_0_fun/gather | solution.py:45
  78.3 4.4 add_multiply_fusion.2
  90.0 3.4 collective-permute-start.2
  97.9 12.0 %collective-permute-done.2 = f32[384,256]{1,0:T(8,128)} collective-permute-done((f32[384,256]{1,0:T(8,128)S(1)}, f32[384,256]{1,0:T(8,128)}, u32[]{:S(2)}, u32[]{:S(2)}) %collective-permute-start.2) | collective-permute-done | bytes 393248 | tf_op jit(solution)/shard_map/ppermute | solution.py:13
  109.9 3.8 scatter_fusion.3
  113.7 3.9 scatter_fusion.4
  117.7 27.1 %fusion = f32[1792,256]{0,1:T(8,128)} fusion(f32[1792,256]{1,0:T(8,128)S(1)} %scatter_fusion.4, f32[1792,1792]{1,0:T(8,128)} %param.11, f32[1792]{0:T(1024)S(1)} %fusion.33), kind=kOutput, calls=%fused_computation.40 | convolution fusion | flops 9865461760 | bytes 16522240 | tf_op jit(solution)/shard_map/dot_general | solution.py:77
  147.5 3.9 gather_fusion.6
  151.3 3.7 gather_fusion.5
  160.3 3.6 collective-permute-start.5
  163.9 10.5 %collective-permute-done.4 = f32[384,256]{1,0:T(8,128)} collective-permute-done((f32[384,256]{1,0:T(8,128)S(1)}, f32[384,256]{1,0:T(8,128)}, u32[]{:S(2)}, u32[]{:S(2)}) %collective-permute-start.4) | collective-permute-done | bytes 393248 | tf_op jit(solution)/shard_map/ppermute | solution.py:13
  174.3 5.6 scatter_fusion.5
  179.9 5.6 scatter_fusion.6
  190.7 41.5 %all-reduce.2 = (f32[256]{0:T(256)S(1)}, f32[256]{0:T(256)S(1)}) all-reduce(f32[256]{0:T(256)S(1)} %get-tuple-element.12, f32[256]{0:T(256)S(1)} %get-tuple-element.11), channel_id=1, replica_groups=mesh['cluster'=4,'sub'=8] {'cluster','sub'}, use_global_device_ids=true, to_apply=%region_9.11 | all-reduce | flops 512 | bytes 4096 | tf_op jit(solution)/shard_map/psum | solution.py:79
  237.7 27.9 %all_to_all.15 = f32[8,128,256]{2,1,0:T(8,128)S(1)} all-to-all(f32[8,128,256]{2,1,0:T(8,128)S(1)} %stack.7), channel_id=1, replica_groups=mesh['cluster'=4,'sub'=8] {'sub'}, dimensions={0} | all-to-all | bytes 2097152 | tf_op jit(solution)/shard_map/all_to_all | solution.py:61
  273.1 3.7 gather_fusion.8
  276.8 3.7 gather_fusion.7
  281.6 3.7 collective-permute-start.6
  289.4 11.8 %collective-permute-done.6 = f32[384,256]{1,0:T(8,128)} collective-permute-done((f32[384,256]{1,0:T(8,128)S(1)}, f32[384,256]{1,0:T(8,128)}, u32[]{:S(2)}, u32[]{:S(2)}) %collective-permute-start.6) | collective-permute-done | bytes 393248 | tf_op jit(solution)/shard_map/ppermute | solution.py:13
  301.3 5.6 scatter_fusion.7
  306.9 5.6 scatter_fusion.8
  312.5 27.7 %fusion.1 = f32[1792,256]{0,1:T(8,128)} fusion(f32[1792,256]{1,0:T(8,128)} %scatter_fusion.8, f32[1792,1792]{1,0:T(8,128)} %param.11, f32[1792]{0:T(1024)S(1)} %fusion.33), kind=kOutput, calls=%fused_computation.41 | convolution fusion | flops 9865461760 | bytes 16522240 | tf_op jit(solution)/shard_map/dot_general | solution.py:77
  343.0 3.9 gather_fusion.10
  346.9 3.7 gather_fusion.9
  355.4 3.9 collective-permute-start.9
  359.4 10.5 %collective-permute-done.8 = f32[384,256]{1,0:T(8,128)} collective-permute-done((f32[384,256]{1,0:T(8,128)S(1)}, f32[384,256]{1,0:T(8,128)}, u32[]{:S(2)}, u32[]{:S(2)}) %collective-permute-start.8) | collective-permute-done | bytes 393248 | tf_op jit(solution)/shard_map/ppermute | solution.py:13
  369.9 5.6 scatter_fusion.9
  375.4 5.6 scatter_fusion.10
  386.2 42.5 %all-reduce.1 = (f32[256]{0:T(256)S(1)}, f32[256]{0:T(256)S(1)}) all-reduce(f32[256]{0:T(256)S(1)} %get-tuple-element.10, f32[256]{0:T(256)S(1)} %get-tuple-element.9), channel_id=1, replica_groups=mesh['cluster'=4,'sub'=8] {'cluster','sub'}, use_global_device_ids=true, to_apply=%region_17.19 | all-reduce | flops 512 | bytes 4096 | tf_op jit(solution)/shard_map/psum | solution.py:79
  434.2 26.7 %all_to_all.16 = f32[8,128,256]{2,1,0:T(8,128)S(1)} all-to-all(f32[8,128,256]{2,1,0:T(8,128)S(1)} %stack.8), channel_id=1, replica_groups=mesh['cluster'=4,'sub'=8] {'sub'}, dimensions={0} | all-to-all | bytes 2097152 | tf_op jit(solution)/shard_map/all_to_all | solution.py:61
  475.6 3.7 collective-permute-start.10
  483.0 12.2 %collective-permute-done.10 = f32[384,256]{1,0:T(8,128)S(1)} collective-permute-done((f32[384,256]{1,0:T(8,128)S(1)}, f32[384,256]{1,0:T(8,128)S(1)}, u32[]{:S(2)}, u32[]{:S(2)}) %collective-permute-start.10) | collective-permute-done | bytes 393248 | tf_op jit(solution)/shard_map/ppermute | solution.py:13
  495.2 5.3 scatter_fusion.11
  500.5 5.3 scatter_fusion.12
  505.9 27.7 %fusion.2 = f32[1792,256]{0,1:T(8,128)} fusion(f32[1792,256]{1,0:T(8,128)} %scatter_fusion.12, f32[1792,1792]{1,0:T(8,128)} %param.11, f32[1792]{0:T(1024)S(1)} %fusion.33), kind=kOutput, calls=%fused_computation.42 | convolution fusion | flops 9865461760 | bytes 16522240 | tf_op jit(solution)/shard_map/dot_general | solution.py:77
  547.2 3.9 collective-permute-start.13
  557.5 4.6 collective-permute-done.12
  562.0 5.1 scatter_fusion.13
  567.2 5.1 scatter_fusion.14
  577.1 42.5 %all-reduce = (f32[256]{0:T(256)S(1)}, f32[256]{0:T(256)S(1)}) all-reduce(f32[256]{0:T(256)S(1)} %get-tuple-element.8, f32[256]{0:T(256)S(1)} %get-tuple-element.7), channel_id=1, replica_groups=mesh['cluster'=4,'sub'=8] {'cluster','sub'}, use_global_device_ids=true, to_apply=%region_25.27 | all-reduce | flops 512 | bytes 4096 | tf_op jit(solution)/shard_map/psum | solution.py:79
  619.7 5.6 multiply_subtract_fusion
  (186 shorter events, 127.2 us)
Async XLA Ops:
  0.6 39.3 %copy-start = (f32[1792,128]{1,0:T(8,128)S(1)}, f32[1792,128]{1,0:T(8,128)}, u32[]{:S(2)}) copy-start(f32[1792,128]{1,0:T(8,128)} %param.12) | copy-start | bytes 2752516
  1.4 4.2 copy-start.28
  4.0 6.1 copy-start.2
  4.0 6.0 copy-start.47
  6.5 21.4 %collective-permute-start = (f32[384,256]{1,0:T(8,128)}, f32[384,256]{1,0:T(8,128)S(1)}, u32[]{:S(2)}, u32[]{:S(2)}) collective-permute-start(f32[384,256]{1,0:T(8,128)} %broadcast_select_fusion.13), channel_id=1, source_target_pairs={{0,1},{1,2},{2,3},{3,4},{4,5},{5,6},{6,7},{7,8},{8,9},{9,10},{10,1... | collective-permute-start | bytes 1179656 | tf_op jit(solution)/shard_map/ppermute | solution.py:13
  11.9 21.1 %collective-permute-start.1 = (f32[384,256]{1,0:T(8,128)S(1)}, f32[384,256]{1,0:T(8,128)S(1)}, u32[]{:S(2)}, u32[]{:S(2)}) collective-permute-start(f32[384,256]{1,0:T(8,128)S(1)} %broadcast_select_fusion.12), channel_id=1, source_target_pairs={{1,0},{2,1},{3,2},{4,3},{5,4},{6,5},{7,6},{8,7},{9,8},{10,9},{11,1... | collective-permute-start | bytes 1179656 | tf_op jit(solution)/shard_map/ppermute | solution.py:13
  15.0 12.9 %copy-start.15 = (s32[384]{0:T(512)}, s32[384]{0:T(512)S(1)}, u32[]{:S(2)}) copy-start(s32[384]{0:T(512)S(1)} %fusion.37) | copy-start | bytes 4612
  19.9 13.2 %copy-start.11 = (s32[384]{0:T(512)}, s32[384]{0:T(512)S(1)}, u32[]{:S(2)}) copy-start(s32[384]{0:T(512)S(1)} %fusion.38) | copy-start | bytes 4612
  42.8 33.7 %all-to-all-start = ((f32[8,128,256]{2,1,0:T(8,128)}), f32[8,128,256]{2,1,0:T(8,128)S(1)}, u32[]{:S(2)}, u32[]{:S(2)}) async-start(f32[8,128,256]{2,1,0:T(8,128)} %stack.6), calls=%async_computation | async-start | bytes 2097152 | tf_op jit(solution)/shard_map/all_to_all | solution.py:61
  48.5 28.0 %copy-start.10 = (f32[128,1024]{1,0:T(8,128)S(1)}, f32[128,1024]{1,0:T(8,128)}, u32[]{:S(2)}) copy-start(f32[128,1024]{1,0:T(8,128)} %param.13) | copy-start | bytes 1572868
  76.5 6.2 copy-start.44
  86.7 6.7 %copy-start.33 = (pred[384]{0:T(512)(128)(4,1)S(1)}, pred[384]{0:T(512)(128)(4,1)}, u32[]{:S(2)}) copy-start(pred[384]{0:T(512)(128)(4,1)} %copy-done.32) | copy-start | bytes 1156
  86.7 23.2 %copy-start.16 = (s32[384]{0:T(512)S(1)}, s32[384]{0:T(512)}, u32[]{:S(2)}) copy-start(s32[384]{0:T(512)} %copy-done.15) | copy-start | bytes 4612
  90.0 19.9 %collective-permute-start.2 = (f32[384,256]{1,0:T(8,128)S(1)}, f32[384,256]{1,0:T(8,128)}, u32[]{:S(2)}, u32[]{:S(2)}) collective-permute-start(f32[384,256]{1,0:T(8,128)S(1)} %broadcast_select_fusion.11), channel_id=1, source_target_pairs={{0,1},{1,2},{2,3},{3,4},{4,5},{5,6},{6,7},{7,8},{8,9},{9,10},{10,1... | collective-permute-start | bytes 1179656 | tf_op jit(solution)/shard_map/ppermute | solution.py:13
  95.3 18.4 %copy-start.12 = (s32[384]{0:T(512)S(1)}, s32[384]{0:T(512)}, u32[]{:S(2)}) copy-start(s32[384]{0:T(512)} %copy-done.11) | copy-start | bytes 4612
  95.3 18.4 %collective-permute-start.3 = (f32[384,256]{1,0:T(8,128)}, f32[384,256]{1,0:T(8,128)}, u32[]{:S(2)}, u32[]{:S(2)}) collective-permute-start(f32[384,256]{1,0:T(8,128)} %broadcast_select_fusion.10), channel_id=1, source_target_pairs={{1,0},{2,1},{3,2},{4,3},{5,4},{6,5},{7,6},{8,7},{9,8},{10,9},{11,1... | collective-permute-start | bytes 1179656 | tf_op jit(solution)/shard_map/ppermute | solution.py:13
  156.1 18.2 %collective-permute-start.4 = (f32[384,256]{1,0:T(8,128)S(1)}, f32[384,256]{1,0:T(8,128)}, u32[]{:S(2)}, u32[]{:S(2)}) collective-permute-start(f32[384,256]{1,0:T(8,128)S(1)} %broadcast_select_fusion.9), channel_id=1, source_target_pairs={{0,1},{1,2},{2,3},{3,4},{4,5},{5,6},{6,7},{7,8},{8,9},{9,10},{10,1... | collective-permute-start | bytes 1179656 | tf_op jit(solution)/shard_map/ppermute | solution.py:13
  160.3 19.7 %collective-permute-start.5 = (f32[384,256]{1,0:T(8,128)}, f32[384,256]{1,0:T(8,128)}, u32[]{:S(2)}, u32[]{:S(2)}) collective-permute-start(f32[384,256]{1,0:T(8,128)} %broadcast_select_fusion.8), channel_id=1, source_target_pairs={{1,0},{2,1},{3,2},{4,3},{5,4},{6,5},{7,6},{8,7},{9,8},{10,9},{11,1... | collective-permute-start | bytes 1179656 | tf_op jit(solution)/shard_map/ppermute | solution.py:13
  232.2 3.5 copy-start.36
  237.5 28.1 %copy-start.37 = (f32[128]{0:T(128)S(1)}, f32[128]{0:T(128)}, u32[]{:S(2)}) copy-start(f32[128]{0:T(128)} %compare_convert_fusion) | copy-start | bytes 1540
  237.6 29.8 %copy-start.5 = (f32[1792,256]{0,1:T(8,128)S(1)}, f32[1792,256]{0,1:T(8,128)}, u32[]{:S(2)}) copy-start(f32[1792,256]{0,1:T(8,128)} %copy-done.4) | copy-start | bytes 5505028
  237.7 29.8 %copy-start.45 = (f32[1792]{0:T(1024)S(1)}, f32[1792]{0:T(1024)}, u32[]{:S(2)}) copy-start(f32[1792]{0:T(1024)} %copy-done.44) | copy-start | bytes 21508
  273.1 3.7 copy-start.21
  276.8 3.7 copy-start.30
  276.8 8.5 %copy-start.34 = (pred[384]{0:T(512)(128)(4,1)S(1)}, pred[384]{0:T(512)(128)(4,1)}, u32[]{:S(2)}) copy-start(pred[384]{0:T(512)(128)(4,1)} %copy-done.32) | copy-start | bytes 1156
  276.8 24.5 %copy-start.17 = (s32[384]{0:T(512)S(1)}, s32[384]{0:T(512)}, u32[]{:S(2)}) copy-start(s32[384]{0:T(512)} %copy-done.15) | copy-start | bytes 4612
  281.6 19.7 %collective-permute-start.6 = (f32[384,256]{1,0:T(8,128)S(1)}, f32[384,256]{1,0:T(8,128)}, u32[]{:S(2)}, u32[]{:S(2)}) collective-permute-start(f32[384,256]{1,0:T(8,128)S(1)} %broadcast_select_fusion.7), channel_id=1, source_target_pairs={{0,1},{1,2},{2,3},{3,4},{4,5},{5,6},{6,7},{7,8},{8,9},{9,10},{10,1... | collective-permute-start | bytes 1179656 | tf_op jit(solution)/shard_map/ppermute | solution.py:13
  287.1 19.7 %copy-start.13 = (s32[384]{0:T(512)S(1)}, s32[384]{0:T(512)}, u32[]{:S(2)}) copy-start(s32[384]{0:T(512)} %copy-done.11) | copy-start | bytes 4612
  287.1 19.7 %collective-permute-start.7 = (f32[384,256]{1,0:T(8,128)}, f32[384,256]{1,0:T(8,128)}, u32[]{:S(2)}, u32[]{:S(2)}) collective-permute-start(f32[384,256]{1,0:T(8,128)} %broadcast_select_fusion.6), channel_id=1, source_target_pairs={{1,0},{2,1},{3,2},{4,3},{5,4},{6,5},{7,6},{8,7},{9,8},{10,9},{11,1... | collective-permute-start | bytes 1179656 | tf_op jit(solution)/shard_map/ppermute | solution.py:13
  351.7 18.2 %collective-permute-start.8 = (f32[384,256]{1,0:T(8,128)S(1)}, f32[384,256]{1,0:T(8,128)}, u32[]{:S(2)}, u32[]{:S(2)}) collective-permute-start(f32[384,256]{1,0:T(8,128)S(1)} %broadcast_select_fusion.5), channel_id=1, source_target_pairs={{0,1},{1,2},{2,3},{3,4},{4,5},{5,6},{6,7},{7,8},{8,9},{9,10},{10,1... | collective-permute-start | bytes 1179656 | tf_op jit(solution)/shard_map/ppermute | solution.py:13
  355.4 20.0 %collective-permute-start.9 = (f32[384,256]{1,0:T(8,128)}, f32[384,256]{1,0:T(8,128)}, u32[]{:S(2)}, u32[]{:S(2)}) collective-permute-start(f32[384,256]{1,0:T(8,128)} %broadcast_select_fusion.4), channel_id=1, source_target_pairs={{1,0},{2,1},{3,2},{4,3},{5,4},{6,5},{7,6},{8,7},{9,8},{10,9},{11,1... | collective-permute-start | bytes 1179656 | tf_op jit(solution)/shard_map/ppermute | solution.py:13
  428.7 3.5 copy-start.38
  434.0 26.8 %copy-start.39 = (f32[128]{0:T(128)S(1)}, f32[128]{0:T(128)}, u32[]{:S(2)}) copy-start(f32[128]{0:T(128)} %compare_convert_fusion) | copy-start | bytes 1540
  434.1 28.5 %copy-start.7 = (f32[1792,256]{0,1:T(8,128)S(1)}, f32[1792,256]{0,1:T(8,128)}, u32[]{:S(2)}) copy-start(f32[1792,256]{0,1:T(8,128)} %copy-done.6) | copy-start | bytes 5505028
  434.2 28.5 %copy-start.46 = (f32[1792]{0:T(1024)S(1)}, f32[1792]{0:T(1024)}, u32[]{:S(2)}) copy-start(f32[1792]{0:T(1024)} %copy-done.44) | copy-start | bytes 21508
  475.6 19.6 %collective-permute-start.10 = (f32[384,256]{1,0:T(8,128)S(1)}, f32[384,256]{1,0:T(8,128)S(1)}, u32[]{:S(2)}, u32[]{:S(2)}) collective-permute-start(f32[384,256]{1,0:T(8,128)S(1)} %broadcast_select_fusion.3), channel_id=1, source_target_pairs={{0,1},{1,2},{2,3},{3,4},{4,5},{5,6},{6,7},{7,8},{8,9},{9,10},{10,1... | collective-permute-start | bytes 1179656 | tf_op jit(solution)/shard_map/ppermute | solution.py:13
  480.8 19.7 %collective-permute-start.11 = (f32[384,256]{1,0:T(8,128)}, f32[384,256]{1,0:T(8,128)S(1)}, u32[]{:S(2)}, u32[]{:S(2)}) collective-permute-start(f32[384,256]{1,0:T(8,128)} %broadcast_select_fusion.2), channel_id=1, source_target_pairs={{1,0},{2,1},{3,2},{4,3},{5,4},{6,5},{7,6},{8,7},{9,8},{10,9},{11,1... | collective-permute-start | bytes 1179656 | tf_op jit(solution)/shard_map/ppermute | solution.py:13
  536.3 3.4 copy-start.22
  539.7 3.2 copy-start.31
  543.7 18.3 %collective-permute-start.12 = (f32[384,256]{1,0:T(8,128)}, f32[384,256]{1,0:T(8,128)S(1)}, u32[]{:S(2)}, u32[]{:S(2)}) collective-permute-start(f32[384,256]{1,0:T(8,128)} %broadcast_select_fusion.1), channel_id=1, source_target_pairs={{0,1},{1,2},{2,3},{3,4},{4,5},{5,6},{6,7},{7,8},{8,9},{9,10},{10,1... | collective-permute-start | bytes 1179656 | tf_op jit(solution)/shard_map/ppermute | solution.py:13
  547.2 20.0 %collective-permute-start.13 = (f32[384,256]{1,0:T(8,128)}, f32[384,256]{1,0:T(8,128)S(1)}, u32[]{:S(2)}, u32[]{:S(2)}) collective-permute-start(f32[384,256]{1,0:T(8,128)} %broadcast_select_fusion), channel_id=1, source_target_pairs={{1,0},{2,1},{3,2},{4,3},{5,4},{6,5},{7,6},{8,7},{9,8},{10,9},{11,1... | collective-permute-start | bytes 1179656 | tf_op jit(solution)/shard_map/ppermute | solution.py:13
  552.8 2.9 copy-start.1
  555.8 6.3 copy-start.18
  557.5 9.7 %copy-start.14 = (s32[384]{0:T(512)S(1)}, s32[384]{0:T(512)}, u32[]{:S(2)}) copy-start(s32[384]{0:T(512)} %copy-done.11) | copy-start | bytes 4612
  572.3 2.9 copy-start.8
  575.2 44.5 %copy-start.41 = (f32[256]{0:T(256)S(1)}, f32[256]{0:T(256)}, u32[]{:S(2)}) copy-start(f32[256]{0:T(256)} %copy-done.40) | copy-start | bytes 3076
  575.2 44.5 %copy-start.43 = (f32[256]{0:T(256)S(1)}, f32[256]{0:T(256)}, u32[]{:S(2)}) copy-start(f32[256]{0:T(256)} %copy-done.42) | copy-start | bytes 3076
  625.3 2.9 copy-start.9
  (15 other events, 31.8 us)
